TPU v7x, 256 devices: a whole 4x4x8 slice. The times are simulated.
256 devices in a mesh: occ: 64 (over x, z, core), aux: 4 (over y).
Axes of the slice: x: 4, y: 4, z: 8, core: 2. Of those that a mesh axis runs over, the one named last changes fastest.
Arguments:
- factors: bfloat16 [128, 256, 1024], P('occ', None, 'aux'), may hold values from -0.8984375 to 0.8984375
- occ_energy: float32 [128], replicated, may hold values from -3 to -0.5
- vir_energy: float32 [256], replicated, may hold values from 0.5 to 3
- i_slot: int32 [2048], P('occ'), may hold values from 0 to 1
- j_slot: int32 [2048], P('occ'), may hold values from 0 to 1
- partner_device: int32 [2048, 1], P('occ'), may hold values from 0 to 63; in each aligned block of 32 rows (0 to 31, 32 to 63, ...) at most 2 rows name the same one
- pair_count: int32 [64], P('occ'), may hold values from 1 to 32, 1843 in all
Outputs:
- gamma: float32 [128, 256, 1024], P('occ', None, 'aux')
- aux_matrix: float32 [1024, 1024], P('aux', 'occ')
Inputs may be any that keep to these rules, and one draw needn't show every extreme that they name: `partner_device`: among the 32 pair slots of one occ index, at most 2 name the same partner device, and some index reaches 2.
All inputs are finite; a program needn't handle non-finite values. No bound on the sum of `pair_count` on one device may be relied on, other than what follows from the above.
Results may differ from a plain program's by a relative error of at most 0.0013.
Values may be sent and summed in bfloat16 or wider, within the bound.
No kernel may reach another device: no remote copies, remote signals or barrier semaphores. Data moves between devices by JAX's collectives and lax.ppermute only.
A program may use at most 128 MiB of HBM per device.

v0:
```python
import jax
import jax.numpy as jnp
from jax import lax
from jax.sharding import PartitionSpec as P


def body(factors, occ_energy, vir_energy, i_slot, j_slot, partner_device, pair_count):
    held, virtuals, columns = factors.shape
    pair_slots = i_slot.shape[0]
    occ_count = lax.axis_size("occ")
    capacity = max(2, (3 * pair_slots // 2 + occ_count - 1) // occ_count)
    slot_total = occ_count * capacity
    device_index = lax.axis_index("occ")
    pair_order = jnp.arange(pair_slots, dtype=jnp.int32)
    living = pair_order < pair_count[0]
    target = partner_device[:, 0]
    earlier = (
        (target[:, None] == target[None, :])
        & living[None, :]
        & (pair_order[None, :] < pair_order[:, None])
    )
    slot_rank = jnp.sum(earlier.astype(jnp.int32), axis=1)
    slot_index = target * capacity + slot_rank
    slot_hit = (slot_index[:, None] == jnp.arange(slot_total, dtype=jnp.int32)[None, :]) & living[
        :, None
    ]
    requests = jnp.sum(jnp.where(slot_hit, j_slot[:, None] + 1, 0), axis=0) - 1
    wanted = lax.all_to_all(requests, "occ", split_axis=0, concat_axis=0, tiled=True)
    wanted_hit = (wanted[:, None] == jnp.arange(held, dtype=jnp.int32)[None, :]).astype(
        jnp.bfloat16
    )
    factor_rows = factors.reshape(held, virtuals * columns)
    far_index = target * held + j_slot
    outgoing = jnp.dot(wanted_hit, factor_rows, preferred_element_type=jnp.float32)
    outgoing = outgoing.astype(jnp.bfloat16).reshape(slot_total, virtuals, columns)
    arrived = lax.all_to_all(outgoing, "occ", split_axis=0, concat_axis=0, tiled=True)
    pick_rows = slot_hit.astype(jnp.bfloat16)
    partner_blocks = jnp.dot(
        pick_rows,
        arrived.reshape(slot_total, virtuals * columns),
        preferred_element_type=jnp.float32,
    )
    partner_blocks = partner_blocks.astype(jnp.bfloat16).reshape(pair_slots, virtuals, columns)
    own_blocks = factors[i_slot]
    orbitals = occ_energy.shape[0]
    table = jnp.arange(orbitals, dtype=jnp.int32)
    own_index = device_index * held + i_slot
    energy_own = jnp.sum(
        jnp.where(own_index[:, None] == table[None, :], occ_energy[None, :], 0.0), axis=1
    )
    energy_far = jnp.sum(
        jnp.where(far_index[:, None] == table[None, :], occ_energy[None, :], 0.0), axis=1
    )
    denominator = (
        vir_energy[None, :, None]
        + vir_energy[None, None, :]
        - energy_own[:, None, None]
        - energy_far[:, None, None]
    )
    partial_value = jnp.einsum(
        "pvq,pwq->pvw", own_blocks, partner_blocks, preferred_element_type=jnp.float32
    )
    summed = lax.psum(partial_value, "aux")
    amplitude = jnp.where(living[:, None, None], summed / denominator, 0.0).astype(jnp.bfloat16)
    local_terms = jnp.einsum(
        "pvw,pwq->pvq", amplitude, partner_blocks, preferred_element_type=jnp.float32
    )
    owner_hit = (i_slot[:, None] == jnp.arange(held, dtype=jnp.int32)[None, :]).astype(jnp.float32)
    gamma_local = jnp.einsum("po,pvq->ovq", owner_hit, local_terms, precision=lax.Precision.HIGHEST)
    return_terms = jnp.einsum(
        "pwv,pwq->pvq", amplitude, own_blocks, preferred_element_type=jnp.float32
    ).astype(jnp.bfloat16)
    placed = jnp.dot(
        slot_hit.astype(jnp.bfloat16).T,
        return_terms.reshape(pair_slots, virtuals * columns),
        preferred_element_type=jnp.float32,
    )
    placed = placed.astype(jnp.bfloat16).reshape(slot_total, virtuals, columns)
    returned = lax.all_to_all(placed, "occ", split_axis=0, concat_axis=0, tiled=True)
    gathered_back = jnp.dot(
        wanted_hit.T,
        returned.reshape(slot_total, virtuals * columns),
        preferred_element_type=jnp.float32,
    )
    gamma = gamma_local + gathered_back.reshape(held, virtuals, columns)
    rounded = gamma.astype(jnp.bfloat16)
    stacked = jnp.stack([rounded, factors])
    gamma_rows = rounded.reshape(held * virtuals, columns)
    factor_flat = factors.reshape(held * virtuals, columns)
    piece = lax.all_gather(stacked, "aux", axis=3, tiled=True)
    width_here = piece.shape[3]
    gamma_piece = piece[0].reshape(held * virtuals, width_here)
    factor_piece = piece[1].reshape(held * virtuals, width_here)
    first = jnp.dot(gamma_rows.T, factor_piece, preferred_element_type=jnp.float32)
    second = jnp.dot(factor_flat.T, gamma_piece, preferred_element_type=jnp.float32)
    terms = first + second
    shared = lax.psum_scatter(terms, "occ", scatter_dimension=1, tiled=True)
    factor_scale = float(orbitals * virtuals) ** (-0.5)
    return (gamma, shared * factor_scale)


def solution(mesh):
    placed = (P("occ", None, "aux"), P(), P(), P("occ"), P("occ"), P("occ", None), P("occ"))
    return jax.shard_map(
        body,
        mesh=mesh,
        in_specs=placed,
        out_specs=(P("occ", None, "aux"), P("aux", "occ")),
        check_vma=False,
    )
```

profile of v0, /device:TPU:8, one launch (start us, length us, event | category | flops | bytes accessed | tf_op | source)
XLA Modules:
  0.0 1268.4 jit_solution(14306813267259421610)
XLA Ops:
  11.0 11.9 all-to-all-start
  24.1 8.2 all-to-all-done
  33.7 8.1 convolution_convert_fusion.1
  41.8 15.6 %copy.41 = bf16[16,8,256,256]{3,2,1,0:T(8,128)(2,1)} copy(bf16[16,8,256,256]{3,1,2,0:T(8,128)(2,1)} %bitcast.69) | data formatting | bytes 33554432
  57.5 6.0 all-to-all-start.1
  66.7 361.4 %all-to-all-done.1 = bf16[128,256,256]{2,1,0:T(8,128)(2,1)} async-done(((bf16[128,256,256]{2,1,0:T(8,128)(2,1)}), bf16[128,256,256]{2,1,0:T(8,128)(2,1)}, u32[]{:S(2)}, u32[]{:S(2)}) %all-to-all-start.1) | async-done | bytes 16777248 | tf_op jit(solution)/shard_map/all_to_all | solution.py:36
  428.1 15.8 %copy.42 = bf16[16,8,256,256]{3,1,2,0:T(8,128)(2,1)S(1)} copy(bf16[16,8,256,256]{3,2,1,0:T(8,128)(2,1)} %bitcast.23) | data formatting | bytes 33554432
  443.9 3.9 convolution_convert_fusion.2
  447.8 3.3 copy.43
  453.1 4.5 fusion.26
  458.6 161.0 %all-reduce.2.cloned.1.call-done = f32[32,256,256]{2,1,0:T(8,128)} async-done(((f32[32,256,256]{2,1,0:T(8,128)}), f32[32,256,256]{2,1,0:T(8,128)}) %all-reduce.2.cloned.1.call-update) | async-done | bytes 8388624 | tf_op jit(solution)/shard_map/psum | solution.py:63
  619.6 5.0 select_convert_fusion
  625.9 4.4 copy.44
  630.3 12.5 convolution_convert_fusion
  642.9 15.6 %copy.45 = bf16[16,8,256,256]{3,2,1,0:T(8,128)(2,1)} copy(bf16[16,8,256,256]{3,1,2,0:T(8,128)(2,1)} %bitcast.68) | data formatting | bytes 33554432
  658.5 10.7 all-to-all-start.2
  669.5 7.9 fusion.27
  677.4 356.4 %all-to-all-done.2 = bf16[128,256,256]{2,1,0:T(8,128)(2,1)} async-done(((bf16[128,256,256]{2,1,0:T(8,128)(2,1)}), bf16[128,256,256]{2,1,0:T(8,128)(2,1)}, u32[]{:S(2)}, u32[]{:S(2)}) %all-to-all-start.2) | async-done | bytes 16777248 | tf_op jit(solution)/shard_map/all_to_all | solution.py:79
  1033.8 23.4 %copy.39 = bf16[128,256,256]{0,2,1:T(8,128)(2,1)} copy(bf16[128,256,256]{2,1,0:T(8,128)(2,1)} %all-to-all-done.2) | data formatting | bytes 33554432 | tf_op jit(solution)/shard_map/reshape | solution.py:82
  1057.3 10.2 fusion
  1067.5 10.6 fusion.25
  1079.7 33.1 %all-gather.2.cloned.1.call-done = bf16[2,2,256,1024]{3,1,2,0:T(2,128)(2,1)} async-done(((bf16[2,2,256,256]{3,1,2,0:T(2,128)(2,1)}), bf16[2,2,256,1024]{3,1,2,0:T(2,128)(2,1)}) %all-gather.2.cloned.1.call-update) | async-done | bytes 2097168 | tf_op jit(solution)/shard_map/all_gather | solution.py:90
  1112.8 2.9 fusion.24
  1119.1 141.2 %reduce-scatter.2.cloned.1.call-done = f32[256,16]{0,1:T(8,128)} async-done(((f32[256,1024]{0,1:T(8,128)}), f32[256,16]{0,1:T(8,128)}) %reduce-scatter.2.cloned.1.call-update) | async-done | bytes 16400 | tf_op jit(solution)/shard_map/reduce_scatter | solution.py:97
  (47 shorter events, 19.8 us)
Async XLA Ops:
  11.0 21.4 %all-to-all-start = ((s32[64,2,1]{1,2,0:T(1,128)}), s32[64,2,1]{1,2,0:T(1,128)S(1)}, u32[]{:S(2)}, u32[]{:S(2)}) async-start(s32[64,2,1]{1,2,0:T(1,128)} %bitcast.5), calls=%async_computation | async-start | bytes 65536 | tf_op jit(solution)/shard_map/all_to_all | solution.py:28
  57.5 6.4 copy-start
  57.5 370.7 %all-to-all-start.1 = ((bf16[128,256,256]{2,1,0:T(8,128)(2,1)}), bf16[128,256,256]{2,1,0:T(8,128)(2,1)}, u32[]{:S(2)}, u32[]{:S(2)}) async-start(bf16[128,256,256]{2,1,0:T(8,128)(2,1)} %bitcast.66), calls=%async_computation.1 | async-start | bytes 33554432 | tf_op jit(solution)/shard_map/all_to_all | solution.py:36
  63.5 556.1 %all-reduce.2.cloned.1.call-start = ((), (), s32[]{:S(2)}) async-start(), calls=%async_computation.4 | async-start | bytes 16777216 | tf_op jit(solution)/shard_map/psum | solution.py:63
  447.8 5.3 copy-start.3
  451.2 1.9 copy-start.2
  457.6 0.7 copy-start.7
  457.6 0.8 copy-start.5
  619.6 5.0 copy-start.4
  624.6 5.7 copy-start.1
  658.5 375.4 %all-to-all-start.2 = ((bf16[128,256,256]{2,1,0:T(8,128)(2,1)}), bf16[128,256,256]{2,1,0:T(8,128)(2,1)}, u32[]{:S(2)}, u32[]{:S(2)}) async-start(bf16[128,256,256]{2,1,0:T(8,128)(2,1)} %bitcast.67), calls=%async_computation.2 | async-start | bytes 33554432 | tf_op jit(solution)/shard_map/all_to_all | solution.py:79
  669.2 443.6 %all-gather.2.cloned.1.call-start = ((), (), s32[]{:S(2)}) async-start(), calls=%async_computation.5 | async-start | bytes 2621440 | tf_op jit(solution)/shard_map/all_gather | solution.py:90
  1057.3 10.2 copy-start.6
  1079.6 180.7 %reduce-scatter.2.cloned.1.call-start = ((), (), s32[]{:S(2)}) async-start(), calls=%async_computation.6 | async-start | bytes 1064960 | tf_op jit(solution)/shard_map/reduce_scatter | solution.py:97
Sparse Core Ops, SparseCore 0:
  457.8 161.7 all-reduce.1
  1079.7 33.0 all-gather.1
  1118.4 141.9 reduce-scatter.1
where the time goes:
time: 1270 us
  waiting for transfers between devices  1060 us (83%)
  local copies, waits for them, and re-layouts  90.8 us (7%)
  matrix products  61 us (5%)
  starting transfers between devices  29.1 us (2%)
  between operations  14.8 us (1%)
    all_to_all x1, waiting for transfers between devices, body(): lax.all_to_all(outgoing, 'occ', split_axis=0, concat_axis=0, tiled=True)  361 us
    all_to_all x1, waiting for transfers between devices, body(): lax.all_to_all(placed, 'occ', split_axis=0, concat_axis=0, tiled=True)  356 us
    psum x1, waiting for transfers between devices, body(): summed = lax.psum(partial_value, 'aux')  161 us
    reduce_scatter x1, waiting for transfers between devices, body(): shared = lax.psum_scatter(terms, 'occ', scatter_dimension=1, tiled=True)  141 us
    unnamed x24, local copies, waits for them, and re-layouts  59.7 us
    all_gather x1, waiting for transfers between devices, body(): piece = lax.all_gather(stacked, 'aux', axis=3, tiled=True)  33.1 us
  transfers between devices with their start and end apart: 6, of which 6 were waited for; matrix products, arithmetic and copies ran while one was open for 1% of the time, Pallas kernels for 0%

commit v1 on v0

--- a/solution.py
+++ b/solution.py
@@ -60,7 +60,9 @@
     partial_value = jnp.einsum(
         "pvq,pwq->pvw", own_blocks, partner_blocks, preferred_element_type=jnp.float32
     )
-    summed = lax.psum(partial_value, "aux")
+    summed = partial_value
+    for hop in (1, 2):
+        summed = summed + lax.ppermute(summed, "aux", [(dev, dev ^ hop) for dev in range(4)])
     amplitude = jnp.where(living[:, None, None], summed / denominator, 0.0).astype(jnp.bfloat16)
     local_terms = jnp.einsum(
         "pvw,pwq->pvq", amplitude, partner_blocks, preferred_element_type=jnp.float32

time: 1270 us -> 1480 us (1.17)
  waiting for transfers between devices: 1060 us -> 1260 us
    ppermute x0 -> x2, waiting for transfers between devices: none -> 361 us  [body(): lax.ppermute(summed, 'aux', [(dev, dev ^ hop) for dev in range(4)])]
    psum x1 -> x0, waiting for transfers between devices: 161 us -> none  [body(): summed = lax.psum(partial_value, 'aux')]
  transfers between devices with their start and end apart: 6 -> 7, of which waited for: 6 -> 7; matrix products, arithmetic and copies ran while one was open for 1% -> 1% of each run, Pallas kernels for 0% -> 0%
where the time goes in v1:
time: 1480 us
  waiting for transfers between devices  1260 us (85%)
  local copies, waits for them, and re-layouts  92.1 us (6%)
  matrix products  57.9 us (4%)
  starting transfers between devices  27.6 us (2%)
  other arithmetic  21.4 us (1%)
  between operations  15.2 us (1%)
    all_to_all x1, waiting for transfers between devices, body(): lax.all_to_all(outgoing, 'occ', split_axis=0, concat_axis=0, tiled=True)  362 us
    ppermute x2, waiting for transfers between devices, body(): lax.ppermute(summed, 'aux', [(dev, dev ^ hop) for dev in range(4)])  361 us
    all_to_all x1, waiting for transfers between devices, body(): lax.all_to_all(placed, 'occ', split_axis=0, concat_axis=0, tiled=True)  356 us
    reduce_scatter x1, waiting for transfers between devices, body(): shared = lax.psum_scatter(terms, 'occ', scatter_dimension=1, tiled=True)  141 us
    unnamed x24, local copies, waits for them, and re-layouts  60.5 us
    all_gather x1, waiting for transfers between devices, body(): piece = lax.all_gather(stacked, 'aux', axis=3, tiled=True)  33.5 us
  transfers between devices with their start and end apart: 7, of which 7 were waited for; matrix products, arithmetic and copies ran while one was open for 1% of the time, Pallas kernels for 0%

profile of v1, /device:TPU:8, one launch (start us, length us, event | category | flops | bytes accessed | tf_op | source)
XLA Modules:
  0.0 1476.4 jit_solution(8039836168822698916)
XLA Ops:
  11.0 11.9 all-to-all-start
  24.1 8.2 all-to-all-done
  33.7 8.2 convolution_convert_fusion.1
  41.9 15.6 %copy.41 = bf16[16,8,256,256]{3,2,1,0:T(8,128)(2,1)} copy(bf16[16,8,256,256]{3,1,2,0:T(8,128)(2,1)} %bitcast.69) | data formatting | bytes 33554432
  57.5 6.5 all-to-all-start.1
  67.0 361.7 %all-to-all-done.1 = bf16[128,256,256]{2,1,0:T(8,128)(2,1)} async-done(((bf16[128,256,256]{2,1,0:T(8,128)(2,1)}), bf16[128,256,256]{2,1,0:T(8,128)(2,1)}, u32[]{:S(2)}, u32[]{:S(2)}) %all-to-all-start.1) | async-done | bytes 16777248 | tf_op jit(solution)/shard_map/all_to_all | solution.py:36
  428.7 15.8 %copy.42 = bf16[16,8,256,256]{3,1,2,0:T(8,128)(2,1)S(1)} copy(bf16[16,8,256,256]{3,2,1,0:T(8,128)(2,1)} %bitcast.23) | data formatting | bytes 33554432
  444.5 3.8 convolution_convert_fusion.2
  448.3 3.3 copy.43
  456.8 180.0 %collective-permute-done = f32[32,256,256]{2,1,0:T(8,128)} collective-permute-done((f32[32,256,256]{2,1,0:T(8,128)S(1)}, f32[32,256,256]{2,1,0:T(8,128)}, u32[]{:S(2)}, u32[]{:S(2)}) %collective-permute-start) | collective-permute-done | bytes 8388640 | tf_op jit(solution)/shard_map/ppermute | solution.py:65
  636.9 10.4 add.68
  650.0 181.4 %collective-permute-done.1 = f32[32,256,256]{2,1,0:T(8,128)S(1)} collective-permute-done((f32[32,256,256]{2,1,0:T(8,128)}, f32[32,256,256]{2,1,0:T(8,128)S(1)}, u32[]{:S(2)}, u32[]{:S(2)}) %collective-permute-start.1) | collective-permute-done | bytes 8388640 | tf_op jit(solution)/shard_map/ppermute | solution.py:65
  831.4 4.7 select_convert_fusion
  837.5 4.4 copy.44
  841.9 12.5 convolution_convert_fusion
  854.4 15.6 %copy.45 = bf16[16,8,256,256]{3,2,1,0:T(8,128)(2,1)} copy(bf16[16,8,256,256]{3,1,2,0:T(8,128)(2,1)} %bitcast.68) | data formatting | bytes 33554432
  870.0 5.9 all-to-all-start.2
  876.5 7.9 fusion.27
  884.5 356.2 %all-to-all-done.2 = bf16[128,256,256]{2,1,0:T(8,128)(2,1)} async-done(((bf16[128,256,256]{2,1,0:T(8,128)(2,1)}), bf16[128,256,256]{2,1,0:T(8,128)(2,1)}, u32[]{:S(2)}, u32[]{:S(2)}) %all-to-all-start.2) | async-done | bytes 16777248 | tf_op jit(solution)/shard_map/all_to_all | solution.py:81
  1240.7 23.8 %copy.39 = bf16[128,256,256]{0,2,1:T(8,128)(2,1)} copy(bf16[128,256,256]{2,1,0:T(8,128)(2,1)} %all-to-all-done.2) | data formatting | bytes 33554432 | tf_op jit(solution)/shard_map/reshape | solution.py:84
  1264.5 10.2 fusion
  1274.7 10.6 fusion.25
  1286.9 33.5 %all-gather.2.cloned.1.call-done = bf16[2,2,256,1024]{3,1,2,0:T(2,128)(2,1)} async-done(((bf16[2,2,256,256]{3,1,2,0:T(2,128)(2,1)}), bf16[2,2,256,1024]{3,1,2,0:T(2,128)(2,1)}) %all-gather.2.cloned.1.call-update) | async-done | bytes 2097168 | tf_op jit(solution)/shard_map/all_gather | solution.py:92
  1326.7 141.2 %reduce-scatter.2.cloned.1.call-done = f32[256,16]{0,1:T(8,128)} async-done(((f32[256,1024]{0,1:T(8,128)}), f32[256,16]{0,1:T(8,128)}) %reduce-scatter.2.cloned.1.call-update) | async-done | bytes 16400 | tf_op jit(solution)/shard_map/reduce_scatter | solution.py:99
  (49 shorter events, 27.6 us)
Async XLA Ops:
  11.0 21.4 %all-to-all-start = ((s32[64,2,1]{1,2,0:T(1,128)}), s32[64,2,1]{1,2,0:T(1,128)S(1)}, u32[]{:S(2)}, u32[]{:S(2)}) async-start(s32[64,2,1]{1,2,0:T(1,128)} %bitcast.5), calls=%async_computation | async-start | bytes 65536 | tf_op jit(solution)/shard_map/all_to_all | solution.py:28
  57.5 6.5 copy-start
  57.5 371.2 %all-to-all-start.1 = ((bf16[128,256,256]{2,1,0:T(8,128)(2,1)}), bf16[128,256,256]{2,1,0:T(8,128)(2,1)}, u32[]{:S(2)}, u32[]{:S(2)}) async-start(bf16[128,256,256]{2,1,0:T(8,128)(2,1)} %bitcast.67), calls=%async_computation.1 | async-start | bytes 33554432 | tf_op jit(solution)/shard_map/all_to_all | solution.py:36
  448.3 3.4 copy-start.3
  451.7 1.9 copy-start.2
  453.6 3.2 copy-start.4
  453.6 196.1 %copy-start.7 = (f32[128]{0:T(128)S(1)}, f32[128]{0:T(128)}, u32[]{:S(2)}) copy-start(f32[128]{0:T(128)} %param.8) | copy-start | bytes 1540
  453.6 196.3 %copy-start.5 = (f32[256]{0:T(256)S(1)}, f32[256]{0:T(256)}, u32[]{:S(2)}) copy-start(f32[256]{0:T(256)} %param.9) | copy-start | bytes 3076
  453.6 183.2 %collective-permute-start = (f32[32,256,256]{2,1,0:T(8,128)S(1)}, f32[32,256,256]{2,1,0:T(8,128)}, u32[]{:S(2)}, u32[]{:S(2)}) collective-permute-start(f32[32,256,256]{2,1,0:T(8,128)S(1)} %fusion.26), channel_id=1, source_target_pairs={{0,1},{1,0},{2,3},{3,2},{4,5},{5,4},{6,7},{7,6},{8,9},{9,8},{10,11... | collective-permute-start | bytes 25165832 | tf_op jit(solution)/shard_map/ppermute | solution.py:65
  647.3 184.1 %collective-permute-start.1 = (f32[32,256,256]{2,1,0:T(8,128)}, f32[32,256,256]{2,1,0:T(8,128)S(1)}, u32[]{:S(2)}, u32[]{:S(2)}) collective-permute-start(f32[32,256,256]{2,1,0:T(8,128)} %add.68), channel_id=1, source_target_pairs={{0,2},{1,3},{2,0},{3,1},{4,6},{5,7},{6,4},{7,5},{8,10},{9,11},{10,... | collective-permute-start | bytes 25165832 | tf_op jit(solution)/shard_map/ppermute | solution.py:65
  836.1 5.8 copy-start.1
  870.0 370.6 %all-to-all-start.2 = ((bf16[128,256,256]{2,1,0:T(8,128)(2,1)}), bf16[128,256,256]{2,1,0:T(8,128)(2,1)}, u32[]{:S(2)}, u32[]{:S(2)}) async-start(bf16[128,256,256]{2,1,0:T(8,128)(2,1)} %bitcast.66), calls=%async_computation.2 | async-start | bytes 33554432 | tf_op jit(solution)/shard_map/all_to_all | solution.py:81
  876.0 444.4 %all-gather.2.cloned.1.call-start = ((), (), s32[]{:S(2)}) async-start(), calls=%async_computation.4 | async-start | bytes 2621440 | tf_op jit(solution)/shard_map/all_gather | solution.py:92
  1264.5 10.2 copy-start.6
  1286.8 181.1 %reduce-scatter.2.cloned.1.call-start = ((), (), s32[]{:S(2)}) async-start(), calls=%async_computation.5 | async-start | bytes 1064960 | tf_op jit(solution)/shard_map/reduce_scatter | solution.py:99
Sparse Core Ops, SparseCore 0:
  1286.9 33.4 all-gather.1
  1326.0 141.9 reduce-scatter.1
